TPU v7x, 256 devices: a whole 4x4x8 slice. The times are simulated.
256 devices in a mesh: row: 128 (over y, z, x), head: 2 (over core).
Axes of the slice: x: 4, y: 4, z: 8, core: 2. Of those that a mesh axis runs over, the one named last changes fastest.
Arguments:
- query_single: bfloat16 [128, 384], P('row'), may hold values from -6 to 6
- key_single: bfloat16 [8192, 384], P('row'), may hold values from -6 to 6
- pair: bfloat16 [128, 8192, 128], P('row'), may hold values from -6 to 32
- query_frames: float32 [12, 128], P(None, 'row'), may hold values from -2.5 to 2.5, as said below
- key_frames: float32 [12, 8192], P(None, 'row'), may hold values from -2.5 to 2.5, as said below
- w_query: bfloat16 [384, 96], P(None, 'head'), may hold values from -0.3125 to 0.3125
- w_key: bfloat16 [384, 96], P(None, 'head'), may hold values from -0.3125 to 0.3125
- w_value: bfloat16 [384, 96], P(None, 'head'), may hold values from -0.3125 to 0.3125
- w_query_points: bfloat16 [384, 72], P(None, 'head'), may hold values from -0.3125 to 0.3125
- w_key_points: bfloat16 [384, 72], P(None, 'head'), may hold values from -0.3125 to 0.3125
- w_value_points: bfloat16 [384, 144], P(None, 'head'), may hold values from -0.3125 to 0.3125
- head_weight: float32 [6], P('head'), may hold values from -2.5 to 0.5
- bias_weight: bfloat16 [6, 128], P('head'), as said below
- w_out: bfloat16 [1056, 384], P('head'), may hold values from -0.1875 to 0.1875
- d_out: bfloat16 [128, 384], P('row'), may hold values from -24 to 24
Outputs:
- output: bfloat16 [128, 384], P('row')
- grad_query: float32 [128, 384], P('row')
- grad_keys: float32 [8192, 384], P('row')
Inputs may be any that keep to these rules, and one draw needn't show every extreme that they name: `bias_weight`: entries within -2.5 and 2.5 over the square root of 128. `query_frames`: rows 0 to 8 of each column form a rotation matrix. `key_frames`: rows 0 to 8 of each column form a rotation matrix.
All inputs are finite; a program needn't handle non-finite values.
Results may differ from a plain program's by a relative error of at most 0.012.
The roundings to bfloat16 on the way count: a program that leaves them out, or rounds other values in their place, can miss the bound.
Values may be sent and summed in bfloat16 or wider, within the bound.
A program may use at most 64 MiB of HBM per device.

v0:
```python
import math
import jax
import jax.numpy as jnp
from jax import lax
from jax.sharding import PartitionSpec as P

C = 16
PQ = 4
PV = 8
LOGIT_SCALE = math.sqrt(1.0 / 3.0)


def point_scale(points):
    return math.sqrt(2.0 / (9.0 * points))


def product(form, former, latter):
    return jnp.einsum(form, former, latter, preferred_element_type=jnp.float32)


def frame_parts(frames):
    columns = frames.shape[1]
    return (frames[:9].reshape(3, 3, columns), frames[9:12])


def rotate(vectors, rotation):
    return jnp.einsum("xyn,nhpy->nhpx", rotation, vectors, precision=lax.Precision.HIGHEST)


def unrotate(vectors, rotation):
    return jnp.einsum("xyn,nhpx->nhpy", rotation, vectors, precision=lax.Precision.HIGHEST)


def split_columns(packed, extents, axis_index):
    pieces = []
    cursor = 0
    for extent in extents:
        pieces.append(lax.slice_in_dim(packed, cursor, cursor + extent, axis=axis_index))
        cursor = cursor + extent
    return pieces


def key_side(key_single, key_frames, w_key, w_value, w_key_points, w_value_points, head_count):
    rows_k = key_single.shape[0]
    rotation, offset = frame_parts(key_frames)
    offset_rows = jnp.transpose(offset)[:, None, None, :]
    keys_b = jnp.dot(key_single, w_key, preferred_element_type=jnp.float32).astype(jnp.bfloat16)
    values_b = jnp.dot(key_single, w_value, preferred_element_type=jnp.float32).astype(jnp.bfloat16)
    local_k = jnp.dot(key_single, w_key_points, preferred_element_type=jnp.float32).reshape(
        rows_k, head_count, PQ, 3
    )
    key_pts = (rotate(local_k, rotation) + offset_rows).astype(jnp.bfloat16).reshape(rows_k, -1)
    local_v = jnp.dot(key_single, w_value_points, preferred_element_type=jnp.float32).reshape(
        rows_k, head_count, PV, 3
    )
    value_pts = (rotate(local_v, rotation) + offset_rows).astype(jnp.bfloat16).reshape(rows_k, -1)
    return (keys_b, values_b, key_pts, value_pts)


def query_pass(
    query_single,
    pair,
    query_frames,
    w_query,
    w_query_points,
    head_weight,
    bias_weight,
    w_out,
    d_out,
    keys_all,
    values_all,
    kp_all,
    vp_all,
):
    rows_q = query_single.shape[0]
    head_count = head_weight.shape[0]
    rotation, offset = frame_parts(query_frames)
    offset_rows = jnp.transpose(offset)[:, None, None, :]
    point_gain = (jax.nn.softplus(head_weight) * point_scale(PQ))[None, :, None]
    query_b = (
        jnp.dot(query_single, w_query, preferred_element_type=jnp.float32)
        .astype(jnp.bfloat16)
        .reshape(rows_q, head_count, C)
    )
    local_q = jnp.dot(query_single, w_query_points, preferred_element_type=jnp.float32).reshape(
        rows_q, head_count, PQ, 3
    )
    query_pts = (
        (rotate(local_q, rotation) + offset_rows)
        .astype(jnp.bfloat16)
        .reshape(rows_q, head_count, 3 * PQ)
    )
    query_sq = jnp.sum(jnp.square(query_pts.astype(jnp.float32)), axis=-1)
    key_sq = jnp.sum(jnp.square(kp_all.astype(jnp.float32)), axis=-1)
    pair_bias = product("hc,qkc->qhk", bias_weight, pair)
    distance = (
        query_sq[:, :, None]
        + jnp.transpose(key_sq)[None, :, :]
        - 2.0 * product("qhe,khe->qhk", query_pts, kp_all)
    )
    logits = LOGIT_SCALE * (
        product("qhc,khc->qhk", query_b, keys_all) / math.sqrt(C)
        + pair_bias
        - 0.5 * point_gain * distance
    )
    attention = jax.nn.softmax(logits, axis=-1)
    attention_b = attention.astype(jnp.bfloat16)
    attended = product("qhk,khc->qhc", attention_b, values_all)
    point_sum = product("qhk,khe->qhe", attention_b, vp_all).reshape(rows_q, head_count, PV, 3)
    pair_out = product("qhk,qkc->qhc", attention_b, pair)
    local_pts = unrotate(point_sum - offset_rows, rotation)
    lengths = jnp.sqrt(1.0 + jnp.sum(jnp.square(local_pts), axis=-1))
    features = jnp.concatenate(
        [attended, local_pts.reshape(rows_q, head_count, 3 * PV), lengths, pair_out], axis=-1
    )
    features = features.astype(jnp.bfloat16).reshape(rows_q, -1)
    output_part = jnp.dot(features, w_out, preferred_element_type=jnp.float32)
    d_features = jnp.dot(d_out, jnp.transpose(w_out), preferred_element_type=jnp.float32).reshape(
        rows_q, head_count, -1
    )
    d_attended = d_features[:, :, :C].astype(jnp.bfloat16)
    d_local = d_features[:, :, C : C + 3 * PV].reshape(rows_q, head_count, PV, 3)
    d_lengths = d_features[:, :, C + 3 * PV : C + 4 * PV]
    d_pair = d_features[:, :, C + 4 * PV :].astype(jnp.bfloat16)
    d_local = d_local + (d_lengths / lengths)[..., None] * local_pts
    d_points = rotate(d_local, rotation).astype(jnp.bfloat16).reshape(rows_q, head_count, 3 * PV)
    d_attention = (
        product("qhc,khc->qhk", d_attended, values_all)
        + product("qhe,khe->qhk", d_points, vp_all)
        + product("qhc,qkc->qhk", d_pair, pair)
    )
    row_total = jnp.sum(attention * d_attention, axis=-1, keepdims=True)
    score_b = (LOGIT_SCALE * attention * (d_attention - row_total)).astype(jnp.bfloat16)
    d_query = product("qhk,khc->qhc", score_b, keys_all) / math.sqrt(C)
    score_rows = jnp.sum(score_b.astype(jnp.float32), axis=-1)[:, :, None]
    d_qpts = point_gain * (
        product("qhk,khe->qhe", score_b, kp_all) - score_rows * query_pts.astype(jnp.float32)
    )
    d_qlocal = (
        unrotate(d_qpts.reshape(rows_q, head_count, PQ, 3), rotation)
        .astype(jnp.bfloat16)
        .reshape(rows_q, -1)
    )
    grad_part = jnp.dot(
        d_query.astype(jnp.bfloat16).reshape(rows_q, -1),
        jnp.transpose(w_query),
        preferred_element_type=jnp.float32,
    )
    grad_part = grad_part + jnp.dot(
        d_qlocal, jnp.transpose(w_query_points), preferred_element_type=jnp.float32
    )
    query_side = jnp.concatenate(
        [
            query_b.reshape(rows_q, -1),
            query_pts.reshape(rows_q, -1),
            d_attended.reshape(rows_q, -1),
            d_points.reshape(rows_q, -1),
        ],
        axis=1,
    )
    return (output_part, grad_part, query_side, attention_b, score_b)


def key_terms(attention_b, score_b, query_side, key_points, point_gain, head_count):
    count_q = query_side.shape[0]
    count_k = key_points.shape[0]
    side_parts = split_columns(
        query_side, [head_count * C, head_count * 3 * PQ, head_count * C, head_count * 3 * PV], 1
    )
    query_b = side_parts[0].reshape(count_q, head_count, C)
    query_pts = side_parts[1].reshape(count_q, head_count, 3 * PQ)
    grad_att = side_parts[2].reshape(count_q, head_count, C)
    grad_pts = side_parts[3].reshape(count_q, head_count, 3 * PV)
    d_key = product("qhk,qhc->khc", score_b, query_b) / math.sqrt(C)
    score_sum = jnp.sum(score_b.astype(jnp.float32), axis=0)
    d_kpts = point_gain * (
        product("qhk,qhe->khe", score_b, query_pts)
        - jnp.transpose(score_sum)[:, :, None] * key_points.astype(jnp.float32)
    )
    d_value = product("qhk,qhc->khc", attention_b, grad_att)
    d_vpts = product("qhk,qhe->khe", attention_b, grad_pts)
    return jnp.concatenate(
        [
            d_key.reshape(count_k, -1),
            d_value.reshape(count_k, -1),
            d_kpts.reshape(count_k, -1),
            d_vpts.reshape(count_k, -1),
        ],
        axis=1,
    )


def key_finish(key_rows, key_frames, w_key, w_value, w_key_points, w_value_points, head_count):
    rows_k = key_rows.shape[0]
    rotation, offset = frame_parts(key_frames)
    pieces = split_columns(
        key_rows, [head_count * C, head_count * C, head_count * 3 * PQ, head_count * 3 * PV], 1
    )
    kp_local = (
        unrotate(pieces[2].reshape(rows_k, head_count, PQ, 3), rotation)
        .astype(jnp.bfloat16)
        .reshape(rows_k, -1)
    )
    vp_local = (
        unrotate(pieces[3].reshape(rows_k, head_count, PV, 3), rotation)
        .astype(jnp.bfloat16)
        .reshape(rows_k, -1)
    )
    result = jnp.dot(
        pieces[0].astype(jnp.bfloat16), jnp.transpose(w_key), preferred_element_type=jnp.float32
    )
    result = result + jnp.dot(
        pieces[1].astype(jnp.bfloat16), jnp.transpose(w_value), preferred_element_type=jnp.float32
    )
    result = result + jnp.dot(
        kp_local, jnp.transpose(w_key_points), preferred_element_type=jnp.float32
    )
    return result + jnp.dot(
        vp_local, jnp.transpose(w_value_points), preferred_element_type=jnp.float32
    )


def shards(
    query_single,
    key_single,
    pair,
    query_frames,
    key_frames,
    w_query,
    w_key,
    w_value,
    w_query_points,
    w_key_points,
    w_value_points,
    head_weight,
    bias_weight,
    w_out,
    d_out,
):
    head_count = head_weight.shape[0]
    keys_b, values_b, key_pts, value_pts = key_side(
        key_single, key_frames, w_key, w_value, w_key_points, w_value_points, head_count
    )
    packed = jnp.concatenate([keys_b, values_b, key_pts, value_pts], axis=1)
    gathered = lax.all_gather(packed, "row", axis=0, tiled=True)
    total_keys = gathered.shape[0]
    pieces = split_columns(
        gathered, [head_count * C, head_count * C, head_count * 3 * PQ, head_count * 3 * PV], 1
    )
    keys_all = pieces[0].reshape(total_keys, head_count, C)
    values_all = pieces[1].reshape(total_keys, head_count, C)
    kp_all = pieces[2].reshape(total_keys, head_count, 3 * PQ)
    vp_all = pieces[3].reshape(total_keys, head_count, 3 * PV)
    output_part, grad_part, query_side, attention_b, score_b = query_pass(
        query_single,
        pair,
        query_frames,
        w_query,
        w_query_points,
        head_weight,
        bias_weight,
        w_out,
        d_out,
        keys_all,
        values_all,
        kp_all,
        vp_all,
    )
    output = lax.psum(output_part, "head").astype(jnp.bfloat16)
    point_gain = (jax.nn.softplus(head_weight) * point_scale(PQ))[None, :, None]
    scores = jnp.concatenate([attention_b, score_b], axis=1)
    rows_n = lax.axis_size("row")
    local_k = key_single.shape[0]
    scores = scores.reshape(2 * head_count, rows_n, local_k)
    scores = lax.all_to_all(scores, "row", split_axis=1, concat_axis=1, tiled=True)
    scores = jnp.transpose(scores, (1, 0, 2))
    side_all = lax.all_gather(query_side, "row", axis=0, tiled=True)
    key_rows = key_terms(
        scores[:, :head_count],
        scores[:, head_count:],
        side_all,
        key_pts.reshape(local_k, head_count, 3 * PQ),
        point_gain,
        head_count,
    )
    grad_keys_part = key_finish(
        key_rows, key_frames, w_key, w_value, w_key_points, w_value_points, head_count
    )
    grad_query, grad_keys = lax.psum((grad_part, grad_keys_part), "head")
    return (output, grad_query, grad_keys)


def solution(mesh):
    return jax.shard_map(
        shards,
        mesh=mesh,
        in_specs=(
            P("row", None),
            P("row", None),
            P("row", None, None),
            P(None, "row"),
            P(None, "row"),
            P(None, "head"),
            P(None, "head"),
            P(None, "head"),
            P(None, "head"),
            P(None, "head"),
            P(None, "head"),
            P("head"),
            P("head", None),
            P("head", None),
            P("row", None),
        ),
        out_specs=(P("row", None), P("row", None), P("row", None)),
        check_vma=False,
    )
```

profile of v0, /device:TPU:1, one launch (start us, length us, event | category | flops | bytes accessed | tf_op | source)
XLA Modules:
  0.0 621.8 jit_solution(9938110551300458424)
XLA Ops:
  10.2 7.5 %fusion.65 = f32[64,3,4,3]{2,3,1,0:T(4,128)S(1)} fusion(f32[64,3,4,3]{3,2,1,0:T(4,128)S(1)} %copy.139, f32[3,3,64,1]{0,1,3,2:T(4,128)S(1)} %copy.198), kind=kOutput, calls=%fused_computation.113 | convolution fusion | flops 82944 | bytes 20736 | tf_op jit(solution)/shard_map/xyn,nhpy->nhpx/dot_general | solution.py:27
  31.2 108.1 %all-gather.3.cloned.1.call-done = bf16[8192,204]{1,0:T(8,128)(2,1)} async-done(((bf16[64,204]{1,0:T(8,128)(2,1)}), bf16[8192,204]{1,0:T(8,128)(2,1)}) %all-gather.3.cloned.1.call-update) | async-done | bytes 3342352 | tf_op jit(solution)/shard_map/all_gather | solution.py:245
  139.3 4.2 slice.77
  143.5 2.9 copy.151
  149.0 4.9 fusion.59
  153.8 2.7 copy.211
  157.9 1.7 fusion.63
  160.6 3.6 slice.78
  164.2 3.8 copy.212
  167.9 1.7 fusion.29
  171.0 1.6 fusion.61
  173.4 1.4 convolution_convert_fusion.6
  179.6 304.1 %all-gather = bf16[128,1,204]{2,1,0:T(2,128)(2,1)} all-gather(bf16[1,1,204]{2,1,0:T(2,128)(2,1)S(1)} %maximum_bitcast_fusion), channel_id=1, replica_groups=mesh['row'=128,'head'=2] {'row'}, dimensions={0}, use_global_device_ids=true | all-gather | bytes 52632 | tf_op jit(solution)/shard_map/all_gather | solution.py:277
  483.6 1.6 copy.163
  487.9 2.2 fusion.70
  490.1 2.6 copy.210
  492.8 1.4 fusion.50
  494.2 1.8 fusion.20
  500.3 6.1 all-to-all-start
  509.0 8.4 %all-to-all-done = bf16[128,2,192]{2,1,0:T(2,128)(2,1)S(1)} async-done(((bf16[128,2,192]{2,1,0:T(2,128)(2,1)}), bf16[128,2,192]{2,1,0:T(2,128)(2,1)S(1)}, u32[]{:S(2)}, u32[]{:S(2)}) %all-to-all-start) | async-done | bytes 98336 | tf_op jit(solution)/shard_map/all_to_all | solution.py:275
  520.6 7.4 %convolution_convert_fusion.1 = bf16[64,3,4,3]{2,3,1,0:T(4,128)(2,1)S(1)} fusion(f32[64,3,4,3]{3,2,1,0:T(4,128)S(1)} %copy.169, f32[3,3,64,1]{0,1,3,2:T(4,128)S(1)} %copy.198), kind=kOutput, calls=%fused_computation.12 | convolution fusion | flops 85248 | bytes 16128 | tf_op jit(solution)/shard_map/xyn,nhpx->nhpy/dot_general | solution.py:31
  530.2 65.1 %all-reduce = (bf16[1,384]{1,0:T(2,128)(2,1)}, f32[1,384]{1,0:T(1,128)}) all-reduce(f32[1,384]{1,0:T(1,128)S(1)} %fusion.69, f32[1,384]{1,0:T(1,128)S(1)} %add.116), channel_id=1, replica_groups=mesh['row'=128,'head'=2] {'head'}, use_global_device_ids=true, to_apply=%region_5.6 | all-reduce | flops 768 | bytes 5376 | tf_op jit(solution)/shard_map/psum | solution.py:269
  595.2 18.1 %all-reduce.3.cloned.1.call-done = f32[64,384]{1,0:T(8,128)} async-done(((f32[64,384]{1,0:T(8,128)}), f32[64,384]{1,0:T(8,128)}) %all-reduce.3.cloned.1.call-update) | async-done | bytes 98320 | tf_op jit(solution)/shard_map/psum | solution.py:289
  613.4 1.5 copy.242
  (177 shorter events, 42.6 us)
Async XLA Ops:
  7.2 150.7 %copy-start = (bf16[1,8192,128]{2,1,0:T(8,128)(2,1)S(1)}, bf16[1,8192,128]{2,1,0:T(8,128)(2,1)}, u32[]{:S(2)}) copy-start(bf16[1,8192,128]{2,1,0:T(8,128)(2,1)} %param.17) | copy-start | bytes 6291460
  7.2 10.8 %copy-start.4 = (bf16[64,384]{1,0:T(8,128)(2,1)S(1)}, bf16[64,384]{1,0:T(8,128)(2,1)}, u32[]{:S(2)}) copy-start(bf16[64,384]{1,0:T(8,128)(2,1)} %param.16) | copy-start | bytes 147460
  7.2 10.8 %copy-start.6 = (bf16[384,72]{0,1:T(8,128)(2,1)S(1)}, bf16[384,72]{0,1:T(8,128)(2,1)}, u32[]{:S(2)}) copy-start(bf16[384,72]{0,1:T(8,128)(2,1)} %param.25) | copy-start | bytes 165892
  7.2 132.1 %all-gather.3.cloned.1.call-start = ((), (), s32[]{:S(2)}) async-start(), calls=%async_computation.1 | async-start | bytes 4227072 | tf_op jit(solution)/shard_map/all_gather | solution.py:245
  8.8 13.5 %copy-start.3 = (bf16[528,384]{1,0:T(8,128)(2,1)S(1)}, bf16[528,384]{1,0:T(8,128)(2,1)}, u32[]{:S(2)}) copy-start(bf16[528,384]{1,0:T(8,128)(2,1)} %param.28) | copy-start | bytes 1216516
  8.8 13.5 %copy-start.25 = (bf16[1,384]{1,0:T(2,128)(2,1)S(1)}, bf16[1,384]{1,0:T(2,128)(2,1)}, u32[]{:S(2)}) copy-start(bf16[1,384]{1,0:T(2,128)(2,1)} %param.29) | copy-start | bytes 2308
  9.9 12.7 %copy-start.29 = (f32[12,1]{0,1:T(1,128)S(1)}, f32[12,1]{0,1:T(1,128)}, u32[]{:S(2)}) copy-start(f32[12,1]{0,1:T(1,128)} %param.18) | copy-start | bytes 148
  10.1 13.4 %copy-start.28 = (bf16[1,384]{1,0:T(2,128)(2,1)S(1)}, bf16[1,384]{1,0:T(2,128)(2,1)}, u32[]{:S(2)}) copy-start(bf16[1,384]{1,0:T(2,128)(2,1)} %param.15) | copy-start | bytes 2308
  10.1 20.5 %copy-start.30 = (f32[3]{0:T(128)S(1)}, f32[3]{0:T(128)}, u32[]{:S(2)}) copy-start(f32[3]{0:T(128)} %param.26) | copy-start | bytes 40
  22.5 121.0 %copy-start.16 = (f32[1,3,176]{2,1,0:T(4,128)}, f32[1,3,176]{2,1,0:T(4,128)S(1)}, u32[]{:S(2)}) copy-start(f32[1,3,176]{2,1,0:T(4,128)S(1)} %copy.189) | copy-start | bytes 6340
  22.6 121.0 %copy-start.18 = (bf16[1,3,176]{2,1,0:T(4,128)(2,1)}, bf16[1,3,176]{2,1,0:T(4,128)(2,1)S(1)}, u32[]{:S(2)}) copy-start(bf16[1,3,176]{2,1,0:T(4,128)(2,1)S(1)} %copy.237) | copy-start | bytes 3172
  27.2 116.3 %copy-start.24 = (bf16[48]{0:T(256)(128)(2,1)}, bf16[48]{0:T(256)(128)(2,1)S(1)}, u32[]{:S(2)}) copy-start(bf16[48]{0:T(256)(128)(2,1)S(1)} %fusion.18) | copy-start | bytes 292
  498.6 8.3 %copy-start.15 = (f32[3,3]{1,0:T(4,128)S(1)}, f32[3,3]{1,0:T(4,128)}, u32[]{:S(2)}) copy-start(f32[3,3]{1,0:T(4,128)} %reshape.334) | copy-start | bytes 112
  498.6 8.9 %copy-start.14 = (bf16[384,48]{0,1:T(8,128)(2,1)S(1)}, bf16[384,48]{0,1:T(8,128)(2,1)}, u32[]{:S(2)}) copy-start(bf16[384,48]{0,1:T(8,128)(2,1)} %param.20) | copy-start | bytes 110596
  498.6 9.0 %copy-start.17 = (bf16[3,8,3]{1,2,0:T(4,128)(2,1)S(1)}, bf16[3,8,3]{1,2,0:T(4,128)(2,1)}, u32[]{:S(2)}) copy-start(bf16[3,8,3]{1,2,0:T(4,128)(2,1)} %get-tuple-element.15) | copy-start | bytes 436
  499.2 20.9 %copy-start.12 = (f32[64,3,4,3]{0,1,3,2:T(4,128)S(1)}, f32[64,3,4,3]{0,1,3,2:T(4,128)}, u32[]{:S(2)}) copy-start(f32[64,3,4,3]{0,1,3,2:T(4,128)} %copy.166) | copy-start | bytes 27652
  499.2 20.9 %copy-start.22 = (f32[3]{0:T(128)S(1)}, f32[3]{0:T(128)}, u32[]{:S(2)}) copy-start(f32[3]{0:T(128)} %get-tuple-element.5) | copy-start | bytes 40
  500.3 17.1 %all-to-all-start = ((bf16[128,2,192]{2,1,0:T(2,128)(2,1)}), bf16[128,2,192]{2,1,0:T(2,128)(2,1)S(1)}, u32[]{:S(2)}, u32[]{:S(2)}) async-start(bf16[128,2,192]{2,1,0:T(2,128)(2,1)} %reshape.419), calls=%async_computation | async-start | bytes 262144 | tf_op jit(solution)/shard_map/all_to_all | solution.py:275
  506.4 107.0 %all-reduce.3.cloned.1.call-start = ((), (), s32[]{:S(2)}) async-start(), calls=%async_computation.2 | async-start | bytes 196608 | tf_op jit(solution)/shard_map/psum | solution.py:289
  508.2 20.3 %copy-start.8 = (bf16[384,48]{0,1:T(8,128)(2,1)S(1)}, bf16[384,48]{0,1:T(8,128)(2,1)}, u32[]{:S(2)}) copy-start(bf16[384,48]{0,1:T(8,128)(2,1)} %param.21) | copy-start | bytes 110596
  509.0 19.7 %copy-start.9 = (bf16[384,48]{0,1:T(8,128)(2,1)S(1)}, bf16[384,48]{0,1:T(8,128)(2,1)}, u32[]{:S(2)}) copy-start(bf16[384,48]{0,1:T(8,128)(2,1)} %param.22) | copy-start | bytes 110596
  517.5 11.4 %copy-start.11 = (bf16[384,36]{0,1:T(8,128)(2,1)S(1)}, bf16[384,36]{0,1:T(8,128)(2,1)}, u32[]{:S(2)}) copy-start(bf16[384,36]{0,1:T(8,128)(2,1)} %param.24) | copy-start | bytes 82948
  517.5 11.6 %copy-start.7 = (bf16[384,72]{0,1:T(8,128)(2,1)S(1)}, bf16[384,72]{0,1:T(8,128)(2,1)}, u32[]{:S(2)}) copy-start(bf16[384,72]{0,1:T(8,128)(2,1)} %param.25) | copy-start | bytes 165892
  518.7 11.3 %copy-start.10 = (bf16[384,36]{0,1:T(8,128)(2,1)S(1)}, bf16[384,36]{0,1:T(8,128)(2,1)}, u32[]{:S(2)}) copy-start(bf16[384,36]{0,1:T(8,128)(2,1)} %param.23) | copy-start | bytes 82948
  (10 other events, 59.1 us)
Sparse Core Ops, SparseCore 0:
  22.4 116.8 all-gather.2
  530.1 83.2 all-reduce.2
where the time goes:
time: 623 us; the launch traced here: 622 us
  blocking collectives  369 us (59%)
  waiting for transfers between devices  135 us (22%)
  local copies, waits for them, and re-layouts  50.5 us (8%)
  matrix products  40.5 us (7%)
  between operations  14.7 us (2%)
  starting transfers between devices  6.41 us (1%)
    all_gather x1, blocking collectives, shards(): side_all = lax.all_gather(query_side, 'row', axis=0, tiled=True)  304 us
    all_gather x1, waiting for transfers between devices, shards(): gathered = lax.all_gather(packed, 'row', axis=0, tiled=True)  108 us
    psum x1, blocking collectives, shards(): output = lax.psum(output_part, 'head').astype(jnp.bfloat16)  65.1 us
    slice x7, local copies, waits for them, and re-layouts, split_columns(): lax.slice_in_dim(packed, cursor, cursor + extent, axis=axis_index)  19 us
    psum x1, waiting for transfers between devices, shards(): grad_query, grad_keys = lax.psum((grad_part, grad_keys_part), 'head')  18.1 us
    dot_general x15, matrix products, product(): return jnp.einsum(form, former, latter, preferred_element_type=jnp.float32)  13.8 us
  transfers between devices with their start and end apart: 3, of which 3 were waited for; matrix products, arithmetic and copies ran while one was open for 2% of the time, Pallas kernels for 0%

commit v1 on v0

--- a/solution.py
+++ b/solution.py
@@ -274,7 +274,9 @@
     scores = scores.reshape(2 * head_count, rows_n, local_k)
     scores = lax.all_to_all(scores, "row", split_axis=1, concat_axis=1, tiled=True)
     scores = jnp.transpose(scores, (1, 0, 2))
-    side_all = lax.all_gather(query_side, "row", axis=0, tiled=True)
+    side_all = jnp.concatenate(
+        lax.all_to_all(jnp.stack([query_side] * lax.axis_size("row")), "row", 0, 0), axis=0
+    )
     key_rows = key_terms(
         scores[:, :head_count],
         scores[:, head_count:],

time: 623 us -> 280 us (0.45)
  blocking collectives: 369 us -> 11 us
  waiting for transfers between devices: 135 us -> 146 us
  starting transfers between devices: 6.41 us -> 15.7 us
    all_gather x1 -> x0, blocking collectives: 304 us -> none  [shards(): side_all = lax.all_gather(query_side, 'row', axis=0, tiled=True)]
    psum x1, blocking collectives: 65.1 us -> 11 us  [shards(): output = lax.psum(output_part, 'head').astype(jnp.bfloat16)]
    all_to_all x0 -> x1, waiting for transfers between devices: none -> 9.41 us  [shards(): lax.all_to_all(jnp.stack([query_side] * lax.axis_size('row')), 'row', 0, 0)]
    all_to_all x0 -> x1, starting transfers between devices: none -> 9.23 us  [shards(): lax.all_to_all(jnp.stack([query_side] * lax.axis_size('row')), 'row', 0, 0)]
  transfers between devices with their start and end apart: 3 -> 4, of which waited for: 3 -> 4; matrix products, arithmetic and copies ran while one was open for 2% -> 4% of each run, Pallas kernels for 0% -> 0%
where the time goes in v1:
time: 280 us; the launch traced here: 279 us
  waiting for transfers between devices  146 us (52%)
  local copies, waits for them, and re-layouts  46.3 us (17%)
  matrix products  39.8 us (14%)
  starting transfers between devices  15.7 us (6%)
  between operations  14.8 us (5%)
  blocking collectives  11 us (4%)
  other arithmetic  5.24 us (2%)
    all_gather x1, waiting for transfers between devices, shards(): gathered = lax.all_gather(packed, 'row', axis=0, tiled=True)  108 us
    psum x1, waiting for transfers between devices, shards(): grad_query, grad_keys = lax.psum((grad_part, grad_keys_part), 'head')  18.1 us
    slice x7, local copies, waits for them, and re-layouts, split_columns(): lax.slice_in_dim(packed, cursor, cursor + extent, axis=axis_index)  15.7 us
    dot_general x15, matrix products, product(): return jnp.einsum(form, former, latter, preferred_element_type=jnp.float32)  13 us
    unnamed x74, local copies, waits for them, and re-layouts  11.9 us
    psum x1, blocking collectives, shards(): output = lax.psum(output_part, 'head').astype(jnp.bfloat16)  11 us
    all_to_all x1, waiting for transfers between devices, shards(): lax.all_to_all(scores, 'row', split_axis=1, concat_axis=1, tiled=True)  10.4 us
    dot_general x4, matrix products, rotate(): jnp.einsum('xyn,nhpy->nhpx', rotation, vectors, precision=lax.Precision.H...  10.4 us
  transfers between devices with their start and end apart: 4, of which 4 were waited for; matrix products, arithmetic and copies ran while one was open for 4% of the time, Pallas kernels for 0%

profile of v1, /device:TPU:1, one launch (start us, length us, event | category | flops | bytes accessed | tf_op | source)
XLA Modules:
  0.0 278.9 jit_solution(2840662058819157597)
XLA Ops:
  10.2 7.5 %fusion.65 = f32[64,3,4,3]{2,3,1,0:T(4,128)S(1)} fusion(f32[64,3,4,3]{3,2,1,0:T(4,128)S(1)} %copy.144, f32[3,3,64,1]{0,1,3,2:T(4,128)S(1)} %copy.203), kind=kOutput, calls=%fused_computation.113 | convolution fusion | flops 82944 | bytes 20736 | tf_op jit(solution)/shard_map/xyn,nhpy->nhpx/dot_general | solution.py:27
  31.2 108.1 %all-gather.2.cloned.1.call-done = bf16[8192,204]{1,0:T(8,128)(2,1)} async-done(((bf16[64,204]{1,0:T(8,128)(2,1)}), bf16[8192,204]{1,0:T(8,128)(2,1)}) %all-gather.2.cloned.1.call-update) | async-done | bytes 3342352 | tf_op jit(solution)/shard_map/all_gather | solution.py:245
  139.3 4.2 %slice.77 = bf16[8192,36]{1,0:T(8,128)(2,1)} slice(bf16[8192,204]{1,0:T(8,128)(2,1)} %all-gather.2.cloned.1.call-done), slice={[0:8192], [96:132]} | slice | bytes 1179648 | tf_op jit(solution)/shard_map/slice | solution.py:38
  143.6 2.9 %copy.156 = bf16[8192,36]{0,1:T(8,128)(2,1)} copy(bf16[8192,36]{1,0:T(8,128)(2,1)} %slice.77) | data formatting | bytes 1179648 | tf_op jit(solution)/shard_map/slice | solution.py:38
  149.0 4.9 %fusion.59 = (bf16[8192,48]{1,0:T(8,128)(2,1)}, bf16[8192,48]{1,0:T(8,128)(2,1)}) fusion(bf16[8192,204]{1,0:T(8,128)(2,1)} %all-gather.2.cloned.1.call-done), kind=kLoop, calls=%fused_computation.106 | loop fusion | bytes 3145728 | tf_op jit(solution)/shard_map/slice | solution.py:38
  153.9 2.7 copy.216
  158.0 1.7 fusion.63
  160.7 3.6 %slice.78 = bf16[8192,72]{1,0:T(8,128)(2,1)} slice(bf16[8192,204]{1,0:T(8,128)(2,1)} %all-gather.2.cloned.1.call-done), slice={[0:8192], [132:204]} | slice | bytes 2359296 | tf_op jit(solution)/shard_map/slice | solution.py:38
  164.2 3.8 %copy.217 = bf16[8192,72]{0,1:T(8,128)(2,1)} copy(bf16[8192,72]{1,0:T(8,128)(2,1)} %slice.78) | data formatting | bytes 2359296
  168.0 1.7 fusion.29
  171.1 1.6 fusion.61
  173.4 1.5 convolution_convert_fusion.6
  178.9 2.2 fusion.70
  181.1 2.6 copy.215
  183.8 1.4 fusion.50
  185.2 1.8 fusion.20
  192.1 9.2 %all-to-all-start = ((bf16[128,1,204]{2,1,0:T(2,128)(2,1)}), bf16[128,1,204]{2,1,0:T(2,128)(2,1)S(1)}, u32[]{:S(2)}, u32[]{:S(2)}) async-start(bf16[128,1,204]{2,1,0:T(2,128)(2,1)} %stack.2), calls=%async_computation | async-start | bytes 262144 | tf_op jit(solution)/shard_map/all_to_all | solution.py:278
  202.9 9.4 %all-to-all-done = bf16[128,1,204]{2,1,0:T(2,128)(2,1)S(1)} async-done(((bf16[128,1,204]{2,1,0:T(2,128)(2,1)}), bf16[128,1,204]{2,1,0:T(2,128)(2,1)S(1)}, u32[]{:S(2)}, u32[]{:S(2)}) %all-to-all-start) | async-done | bytes 52256 | tf_op jit(solution)/shard_map/all_to_all | solution.py:278
  212.3 6.1 %all-to-all-start.1 = ((bf16[128,2,192]{2,1,0:T(2,128)(2,1)}), bf16[128,2,192]{2,1,0:T(2,128)(2,1)S(1)}, u32[]{:S(2)}, u32[]{:S(2)}) async-start(bf16[128,2,192]{2,1,0:T(2,128)(2,1)} %reshape.425), calls=%async_computation.1 | async-start | bytes 262144 | tf_op jit(solution)/shard_map/all_to_all | solution.py:275
  219.0 10.4 %all-to-all-done.1 = bf16[128,2,192]{2,1,0:T(2,128)(2,1)S(1)} async-done(((bf16[128,2,192]{2,1,0:T(2,128)(2,1)}), bf16[128,2,192]{2,1,0:T(2,128)(2,1)S(1)}, u32[]{:S(2)}, u32[]{:S(2)}) %all-to-all-start.1) | async-done | bytes 98336 | tf_op jit(solution)/shard_map/all_to_all | solution.py:275
  231.9 7.4 %convolution_convert_fusion.1 = bf16[64,3,4,3]{2,3,1,0:T(4,128)(2,1)S(1)} fusion(f32[64,3,4,3]{3,2,1,0:T(4,128)S(1)} %copy.174, f32[3,3,64,1]{0,1,3,2:T(4,128)S(1)} %copy.203), kind=kOutput, calls=%fused_computation.12 | convolution fusion | flops 85248 | bytes 16128 | tf_op jit(solution)/shard_map/xyn,nhpx->nhpy/dot_general | solution.py:31
  241.5 11.0 %all-reduce = (bf16[1,384]{1,0:T(2,128)(2,1)}, f32[1,384]{1,0:T(1,128)}) all-reduce(f32[1,384]{1,0:T(1,128)S(1)} %fusion.69, f32[1,384]{1,0:T(1,128)S(1)} %add.116), channel_id=1, replica_groups=mesh['row'=128,'head'=2] {'head'}, use_global_device_ids=true, to_apply=%region_5.6 | all-reduce | flops 768 | bytes 5376 | tf_op jit(solution)/shard_map/psum | solution.py:269
  252.5 18.1 %all-reduce.3.cloned.1.call-done = f32[64,384]{1,0:T(8,128)} async-done(((f32[64,384]{1,0:T(8,128)}), f32[64,384]{1,0:T(8,128)}) %all-reduce.3.cloned.1.call-update) | async-done | bytes 98320 | tf_op jit(solution)/shard_map/psum | solution.py:291
  270.6 1.5 copy.247
  (185 shorter events, 38.7 us)
Async XLA Ops:
  7.2 150.8 %copy-start = (bf16[1,8192,128]{2,1,0:T(8,128)(2,1)S(1)}, bf16[1,8192,128]{2,1,0:T(8,128)(2,1)}, u32[]{:S(2)}) copy-start(bf16[1,8192,128]{2,1,0:T(8,128)(2,1)} %param.17) | copy-start | bytes 6291460
  7.2 132.1 %all-gather.2.cloned.1.call-start = ((), (), s32[]{:S(2)}) async-start(), calls=%async_computation.2 | async-start | bytes 4227072 | tf_op jit(solution)/shard_map/all_gather | solution.py:245
  8.8 13.5 %copy-start.3 = (bf16[528,384]{1,0:T(8,128)(2,1)S(1)}, bf16[528,384]{1,0:T(8,128)(2,1)}, u32[]{:S(2)}) copy-start(bf16[528,384]{1,0:T(8,128)(2,1)} %param.28) | copy-start | bytes 1216516
  8.8 13.5 %copy-start.27 = (bf16[1,384]{1,0:T(2,128)(2,1)S(1)}, bf16[1,384]{1,0:T(2,128)(2,1)}, u32[]{:S(2)}) copy-start(bf16[1,384]{1,0:T(2,128)(2,1)} %param.29) | copy-start | bytes 2308
  9.9 12.7 %copy-start.32 = (f32[12,1]{0,1:T(1,128)S(1)}, f32[12,1]{0,1:T(1,128)}, u32[]{:S(2)}) copy-start(f32[12,1]{0,1:T(1,128)} %param.18) | copy-start | bytes 148
  10.1 13.4 %copy-start.31 = (bf16[1,384]{1,0:T(2,128)(2,1)S(1)}, bf16[1,384]{1,0:T(2,128)(2,1)}, u32[]{:S(2)}) copy-start(bf16[1,384]{1,0:T(2,128)(2,1)} %param.15) | copy-start | bytes 2308
  10.1 20.5 %copy-start.33 = (f32[3]{0:T(128)S(1)}, f32[3]{0:T(128)}, u32[]{:S(2)}) copy-start(f32[3]{0:T(128)} %param.26) | copy-start | bytes 40
  22.5 121.0 %copy-start.15 = (f32[1,3,176]{2,1,0:T(4,128)}, f32[1,3,176]{2,1,0:T(4,128)S(1)}, u32[]{:S(2)}) copy-start(f32[1,3,176]{2,1,0:T(4,128)S(1)} %copy.194) | copy-start | bytes 6340
  22.6 121.0 %copy-start.17 = (bf16[1,3,176]{2,1,0:T(4,128)(2,1)}, bf16[1,3,176]{2,1,0:T(4,128)(2,1)S(1)}, u32[]{:S(2)}) copy-start(bf16[1,3,176]{2,1,0:T(4,128)(2,1)S(1)} %copy.242) | copy-start | bytes 3172
  27.3 116.3 %copy-start.24 = (bf16[48]{0:T(256)(128)(2,1)}, bf16[48]{0:T(256)(128)(2,1)S(1)}, u32[]{:S(2)}) copy-start(bf16[48]{0:T(256)(128)(2,1)S(1)} %fusion.18) | copy-start | bytes 292
  189.6 11.8 %copy-start.19 = (bf16[3,12]{1,0:T(4,128)(2,1)S(1)}, bf16[3,12]{1,0:T(4,128)(2,1)}, u32[]{:S(2)}) copy-start(bf16[3,12]{1,0:T(4,128)(2,1)} %reshape.342) | copy-start | bytes 220
  189.6 11.8 %copy-start.20 = (f32[3]{0:T(128)S(1)}, f32[3]{0:T(128)}, u32[]{:S(2)}) copy-start(f32[3]{0:T(128)} %get-tuple-element.5) | copy-start | bytes 40
  189.6 11.8 %copy-start.22 = (f32[3]{0:T(128)S(1)}, f32[3]{0:T(128)}, u32[]{:S(2)}) copy-start(f32[3]{0:T(128)} %get-tuple-element.7) | copy-start | bytes 40
  189.6 11.8 %copy-start.28 = (f32[3,1,12]{2,1,0:T(1,128)S(1)}, f32[3,1,12]{2,1,0:T(1,128)}, u32[]{:S(2)}) copy-start(f32[3,1,12]{2,1,0:T(1,128)} %fusion.25) | copy-start | bytes 436
  189.6 11.9 %copy-start.14 = (f32[3,3]{1,0:T(4,128)S(1)}, f32[3,3]{1,0:T(4,128)}, u32[]{:S(2)}) copy-start(f32[3,3]{1,0:T(4,128)} %reshape.340) | copy-start | bytes 112
  189.6 12.6 %copy-start.16 = (bf16[3,8,3]{1,2,0:T(4,128)(2,1)S(1)}, bf16[3,8,3]{1,2,0:T(4,128)(2,1)}, u32[]{:S(2)}) copy-start(bf16[3,8,3]{1,2,0:T(4,128)(2,1)} %get-tuple-element.15) | copy-start | bytes 436
  189.7 13.1 %copy-start.13 = (bf16[384,48]{0,1:T(8,128)(2,1)S(1)}, bf16[384,48]{0,1:T(8,128)(2,1)}, u32[]{:S(2)}) copy-start(bf16[384,48]{0,1:T(8,128)(2,1)} %param.20) | copy-start | bytes 110596
  190.4 41.1 %copy-start.12 = (f32[64,3,4,3]{0,1,3,2:T(4,128)S(1)}, f32[64,3,4,3]{0,1,3,2:T(4,128)}, u32[]{:S(2)}) copy-start(f32[64,3,4,3]{0,1,3,2:T(4,128)} %copy.171) | copy-start | bytes 27652
  190.4 41.1 %copy-start.21 = (f32[3]{0:T(128)S(1)}, f32[3]{0:T(128)}, u32[]{:S(2)}) copy-start(f32[3]{0:T(128)} %get-tuple-element.5) | copy-start | bytes 40
  192.1 20.2 %all-to-all-start = ((bf16[128,1,204]{2,1,0:T(2,128)(2,1)}), bf16[128,1,204]{2,1,0:T(2,128)(2,1)S(1)}, u32[]{:S(2)}, u32[]{:S(2)}) async-start(bf16[128,1,204]{2,1,0:T(2,128)(2,1)} %stack.2), calls=%async_computation | async-start | bytes 262144 | tf_op jit(solution)/shard_map/all_to_all | solution.py:278
  212.3 17.1 %all-to-all-start.1 = ((bf16[128,2,192]{2,1,0:T(2,128)(2,1)}), bf16[128,2,192]{2,1,0:T(2,128)(2,1)S(1)}, u32[]{:S(2)}, u32[]{:S(2)}) async-start(bf16[128,2,192]{2,1,0:T(2,128)(2,1)} %reshape.425), calls=%async_computation.1 | async-start | bytes 262144 | tf_op jit(solution)/shard_map/all_to_all | solution.py:275
  218.5 52.1 %all-reduce.3.cloned.1.call-start = ((), (), s32[]{:S(2)}) async-start(), calls=%async_computation.3 | async-start | bytes 196608 | tf_op jit(solution)/shard_map/psum | solution.py:291
  218.9 21.0 %copy-start.8 = (bf16[384,48]{0,1:T(8,128)(2,1)S(1)}, bf16[384,48]{0,1:T(8,128)(2,1)}, u32[]{:S(2)}) copy-start(bf16[384,48]{0,1:T(8,128)(2,1)} %param.21) | copy-start | bytes 110596
  218.9 21.1 %copy-start.9 = (bf16[384,48]{0,1:T(8,128)(2,1)S(1)}, bf16[384,48]{0,1:T(8,128)(2,1)}, u32[]{:S(2)}) copy-start(bf16[384,48]{0,1:T(8,128)(2,1)} %param.22) | copy-start | bytes 110596
  (14 other events, 81.3 us)
Sparse Core Ops, SparseCore 0:
  22.4 116.8 all-gather.1
  241.4 29.0 all-reduce.2
